TPU v7x, 32 devices: a whole 2x2x4 slice. The times are simulated.
32 devices in a mesh: ad: 8 (over z, core), tp: 4 (over y, x).
Axes of the slice: x: 2, y: 2, z: 4, core: 2. Of those that a mesh axis runs over, the one named last changes fastest.
Arguments:
- tokens: bfloat16 [1024, 8192], P('ad', 'tp'), may hold values from -6 to 6
- query_weight: bfloat16 [8192, 8192], P(None, 'tp'), may hold values from -0.0625 to 0.0625
- adapter_down_weight: bfloat16 [128, 8192, 64], P('ad', 'tp'), may hold values from -0.0625 to 0.0625
- adapter_up_weight: bfloat16 [128, 64, 8192], P('ad', None, 'tp'), may hold values from -0.75 to 0.75
- row_adapter_index: int32 [1024], P('ad'), may hold values from 0 to 127, as said below
- adapter_table_slot: int32 [128], replicated, may hold values from 0 to 127, as said below
- lengths: int32 [1024], P('ad'), may hold values from 1 to 64, as said below
- cached_key_rows: bfloat16 [1024, 8, 64, 128], P('ad', None, 'tp'), may hold values from -360 to 360
- cached_value_rows: bfloat16 [1024, 8, 64, 128], P('ad', None, 'tp'), may hold values from -6 to 6
Outputs:
- queries: bfloat16 [1024, 8192], P('ad', 'tp')
- attended: bfloat16 [1024, 8192], P('ad', 'tp')
Inputs may be any that keep to these rules, and one draw needn't show every extreme that they name: `row_adapter_index`: within each aligned block of 128 rows at most 48 rows have their adapter's slot in any one run of 16 slots (slot // 16); one such run, drawn from the seed, is named by exactly 48 rows of every block. `adapter_table_slot`: A permutation of the slots. `lengths`: some row has exactly 64 and some row exactly 1.
All inputs are finite; a program needn't handle non-finite values.
Results may differ from a plain program's by a relative error of at most 0.019.
Values may be sent and summed in bfloat16 or wider, within the bound.
A program may use at most 128 MiB of HBM per device.

v0:
```python
import math

import jax
import jax.numpy as jnp
from jax import lax
from jax.sharding import PartitionSpec as P


def rotate(query, lengths):
    head_dim = query.shape[-1]
    half = head_dim // 2
    freq = jnp.exp(jnp.arange(half, dtype=jnp.float32) * (-2.0 * math.log(500000.0) / head_dim))
    angle = (lengths - 1).astype(jnp.float32)[:, None, None] * freq[None, None, :]
    cosine = jnp.cos(angle)
    sine = jnp.sin(angle)
    first = query[..., :half]
    second = query[..., half:]
    return jnp.concatenate(
        [first * cosine - second * sine, second * cosine + first * sine], axis=-1
    )


def lookup(ids, adapter_table_slot):
    table = jnp.arange(adapter_table_slot.shape[0], dtype=jnp.int32)
    return jnp.sum(
        jnp.where(ids[:, None] == table[None, :], adapter_table_slot[None, :], 0), axis=1
    )


def shrink_rows(input_rows, local_partial, adapter_down_weight):
    adapter_row_count = adapter_down_weight.shape[0]
    select_rows = (
        local_partial[:, None] == jnp.arange(adapter_row_count, dtype=jnp.int32)[None, :]
    ).astype(jnp.float32)
    update_terms = jnp.einsum(
        "nt,vtm->nvm", input_rows, adapter_down_weight, preferred_element_type=jnp.float32
    )
    return (select_rows, jnp.sum(update_terms * select_rows[:, :, None], axis=1))


def expand_rows(select_rows, reduced_rows, adapter_up_weight):
    spread_rows = (select_rows[:, :, None] * reduced_rows.astype(jnp.float32)[:, None, :]).astype(
        jnp.bfloat16
    )
    return jnp.einsum(
        "pow,owu->pu", spread_rows, adapter_up_weight, preferred_element_type=jnp.float32
    ).astype(jnp.bfloat16)


def per_device(
    tokens,
    query_weight,
    adapter_down_weight,
    adapter_up_weight,
    row_adapter_index,
    adapter_table_slot,
    lengths,
    cached_key_rows,
    cached_value_rows,
):
    rows = tokens.shape[0]
    columns = query_weight.shape[1]
    tp_count = lax.axis_size("tp")
    owner_partials = adapter_down_weight.shape[0]
    base = jnp.dot(
        lax.all_gather(tokens, "tp", axis=1, tiled=True),
        query_weight,
        preferred_element_type=jnp.float32,
    )
    combined_output, every_id = (
        lax.all_gather(tokens, "ad", axis=0, tiled=True),
        lax.all_gather(row_adapter_index, "ad", axis=0, tiled=True),
    )
    slots = lookup(every_id, adapter_table_slot)
    mine = slots // owner_partials == lax.axis_index("ad")
    local_partial = jnp.where(mine, slots % owner_partials, -1)
    select_rows, partial_value_sum = shrink_rows(
        combined_output, local_partial, adapter_down_weight
    )
    reduced_rows = lax.psum(partial_value_sum, "tp").astype(jnp.bfloat16)
    lowrank_change = expand_rows(select_rows, reduced_rows, adapter_up_weight)
    delta = lax.psum_scatter(
        lowrank_change.astype(jnp.float32).astype(jnp.bfloat16),
        "ad",
        scatter_dimension=0,
        tiled=True,
    ).astype(jnp.float32)
    head_dim = cached_key_rows.shape[3]
    query = (base + delta).reshape(rows, columns // head_dim, head_dim)
    queries = rotate(query, lengths).reshape(rows, columns).astype(jnp.bfloat16)
    every_head = lax.all_gather(queries, "tp", axis=1, tiled=True)
    kv_heads = cached_key_rows.shape[1]
    span = cached_key_rows.shape[2]
    grouped = every_head.reshape(rows, kv_heads, -1, head_dim)
    scores = jnp.einsum(
        "rkgd,rkpd->rkgp", grouped, cached_key_rows, preferred_element_type=jnp.float32
    ) * (1.0 / math.sqrt(head_dim))
    position = lax.axis_index("tp") * span + jnp.arange(span, dtype=jnp.int32)
    valid = (position[None, :] < lengths[:, None])[:, None, None, :]
    scores = jnp.where(valid, scores, -1e30)
    peak = jnp.max(scores, axis=-1)
    weights = jnp.where(valid, jnp.exp(scores - peak[..., None]), 0.0)
    total = jnp.sum(weights, axis=-1)
    partial_out = jnp.einsum(
        "rkgp,rkpd->rkgd",
        weights.astype(jnp.bfloat16),
        cached_value_rows,
        preferred_element_type=jnp.float32,
    ).astype(jnp.bfloat16)
    peaks, totals = (
        lax.all_to_all(
            peak.reshape(rows, tp_count, -1), "tp", split_axis=1, concat_axis=1, tiled=True
        ),
        lax.all_to_all(
            total.reshape(rows, tp_count, -1), "tp", split_axis=1, concat_axis=1, tiled=True
        ),
    )
    partials = lax.all_to_all(
        partial_out.reshape(rows, tp_count, -1), "tp", split_axis=1, concat_axis=1, tiled=True
    )
    highest = jnp.max(peaks, axis=1, keepdims=True)
    factor = jnp.exp(peaks - highest)
    numer = jnp.sum(
        factor[..., None] * partials.reshape(rows, tp_count, -1, head_dim).astype(jnp.float32),
        axis=1,
    )
    denom = jnp.sum(factor * totals, axis=1)
    attended = (numer / denom[..., None]).reshape(rows, columns).astype(jnp.bfloat16)
    return (queries, attended)


def solution(mesh):
    return jax.shard_map(
        per_device,
        mesh=mesh,
        in_specs=(
            P("ad", "tp"),
            P(None, "tp"),
            P("ad", "tp", None),
            P("ad", None, "tp"),
            P("ad"),
            P(),
            P("ad"),
            P("ad", None, "tp", None),
            P("ad", None, "tp", None),
        ),
        out_specs=(P("ad", "tp"), P("ad", "tp")),
        check_vma=False,
    )
```

profile of v0, /device:TPU:0, one launch (start us, length us, event | category | flops | bytes accessed | tf_op | source)
XLA Modules:
  0.0 274.9 jit_solution(6826846657034868188)
XLA Ops:
  8.7 13.5 %all-gather = s32[8,1,128]{2,1,0:T(1,128)S(1)} all-gather(s32[1,1,128]{2,1,0:T(1,128)} %bitcast.48), channel_id=1, replica_groups=mesh['ad'=8,'tp'=4] {'ad'}, dimensions={0}, use_global_device_ids=true | all-gather | bytes 4608 | tf_op jit(solution)/shard_map/all_gather | solution.py:72
  22.2 1.0 select_reduce_fusion
  23.3 36.2 %all-gather.7.cloned.1.call-done = bf16[1024,2048]{1,0:T(8,128)(2,1)} async-done(((bf16[128,2048]{1,0:T(8,128)(2,1)}), bf16[1024,2048]{1,0:T(8,128)(2,1)}) %all-gather.7.cloned.1.call-update) | async-done | bytes 4194320 | tf_op jit(solution)/shard_map/all_gather | solution.py:71
  59.5 7.6 %fusion.25 = f32[1024,1024]{0,1:S(1)} fusion(bf16[1024,2048]{1,0:T(8,128)(2,1)} %all-gather.7.cloned.1.call-done, bf16[2048,1024]{0,1:T(8,128)(2,1)} %bitcast.49), kind=kOutput, calls=%fused_computation.52 | convolution fusion | flops 4294967296 | bytes 12582912
  67.6 25.3 %all-reduce.1 = bf16[1024,64]{0,1:T(8,128)(2,1)S(1)} all-reduce(f32[1024,64]{0,1:T(8,128)S(1)} %multiply_reduce_fusion.1), channel_id=1, replica_groups=mesh['ad'=8,'tp'=4] {'tp'}, use_global_device_ids=true, to_apply=%region_2.3 | all-reduce | flops 65536 | bytes 393216 | tf_op jit(solution)/shard_map/psum | solution.py:80
  93.0 8.3 %bitcast_convert_fusion = bf16[1024,2048]{1,0:T(8,128)(2,1)} fusion(bf16[16,64,2048]{2,1,0:T(8,128)(2,1)} %param.12, f32[1024,64]{0,1:T(8,128)S(1)} %convert_element_type.71, f32[1024,16]{0,1:T(8,128)S(1)} %fusion.17), kind=kOutput, calls=%fused_computation | convolution fusion | flops 4299161600 | bytes 8716288 | tf_op jit(solution)/shard_map/pow,owu->pu/dot_general | solution.py:45
  102.3 49.9 %reduce-scatter.2.cloned.1.call-done = bf16[128,2048]{1,0:T(8,128)(2,1)} async-done(((bf16[1024,2048]{1,0:T(8,128)(2,1)}), bf16[128,2048]{1,0:T(8,128)(2,1)}) %reduce-scatter.2.cloned.1.call-update) | async-done | bytes 524304 | tf_op jit(solution)/shard_map/reduce_scatter | solution.py:82
  152.1 15.7 %fusion.15 = f32[16,8,16,128]{3,1,2,0:T(8,128)S(1)} fusion(bf16[128,8192]{1,0:T(8,128)(2,1)} %all-gather.5.cloned.1.call-done, bf16[8192,2048]{1,0:T(8,128)(2,1)} %param.10, bf16[128,2048]{1,0:T(8,128)(2,1)} %reduce-scatter.2.cloned.1.call-done), kind=kOutput, calls=%fused_computation.19 | convolution fusion | flops 4295491584 | bytes 37224448 | tf_op jit(solution)/shard_map/dot_general | solution.py:65
  168.9 0.9 copy.29
  169.9 33.5 %all-gather.9.cloned.1.call-done = bf16[128,8192]{1,0:T(8,128)(2,1)} async-done(((bf16[128,2048]{1,0:T(8,128)(2,1)}), bf16[128,8192]{1,0:T(8,128)(2,1)}) %all-gather.9.cloned.1.call-update) | async-done | bytes 2097168 | tf_op jit(solution)/shard_map/all_gather | solution.py:91
  203.4 2.3 copy.25
  206.3 4.2 %fusion = (f32[128,8,8]{2,1,0:T(8,128)S(1)}, f32[128,8,8,16]{3,2,1,0:T(8,128)}) fusion(pred[128,16]{1,0:T(8,128)(4,1)S(1)} %broadcast_compare_fusion, bf16[128,8,8,128]{3,2,1,0:T(8,128)(2,1)S(1)} %bitcast.40, bf16[128,8,16,128]{3,2,1,0:T(8,128)(2,1)S(1)} %copy-done), kind=kOutput, calls=%fused_computation.6 | convolution fusion | flops 33939456 | bytes 6850560 | tf_op jit(solution)/shard_map/rkgd,rkpd->rkgp/dot_general | solution.py:95
  211.3 3.3 %all-to-all-start = ((f32[128,4,16]{0,2,1:T(8,128)}), f32[128,4,16]{0,2,1:T(8,128)S(1)}, u32[]{:S(2)}, u32[]{:S(2)}) async-start(f32[128,4,16]{0,2,1:T(8,128)} %bitcast.6), calls=%async_computation.1 | async-start | bytes 65536 | tf_op jit(solution)/shard_map/all_to_all | solution.py:111
  214.6 4.7 %fusion.1 = f32[128,8,8]{2,1,0:T(8,128)S(1)} fusion(f32[128,8,8,16]{3,2,1,0:T(8,128)} %get-tuple-element.9, f32[128,8,8]{2,1,0:T(8,128)S(1)} %get-tuple-element.8, pred[128,16]{1,0:T(8,128)(4,1)S(1)} %broadcast_compare_fusion), kind=kLoop, calls=%fused_computation.7 | loop fusion | flops 647168 | bytes 591872 | tf_op jit(solution)/shard_map/reduce_sum | solution.py:103
  220.1 4.2 %all-to-all-start.2 = ((f32[128,4,16]{0,2,1:T(8,128)}), f32[128,4,16]{0,2,1:T(8,128)S(1)}, u32[]{:S(2)}, u32[]{:S(2)}) async-start(f32[128,4,16]{0,2,1:T(8,128)} %bitcast.7), calls=%async_computation.3 | async-start | bytes 65536 | tf_op jit(solution)/shard_map/all_to_all | solution.py:114
  224.3 6.4 %fusion.12 = bf16[128,8,8,128]{3,2,1,0:T(8,128)(2,1)} fusion(bf16[128,8,16,128]{3,2,1,0:T(8,128)(2,1)} %param.17, f32[128,8,8,16]{3,2,1,0:T(8,128)} %get-tuple-element.9, f32[128,8,8]{2,1,0:T(8,128)S(1)} %get-tuple-element.8, pred[128,16]{1,0:T(8,128)(4,1)S(1)} %broadcast_compare_fusion), kind=kOutput, calls=%fused_computation.18 | convolution fusion | flops 35258368 | bytes 6850560 | tf_op jit(solution)/shard_map/rkgp,rkpd->rkgd/dot_general | solution.py:104
  230.6 2.5 reshape.175
  233.2 2.5 copy.20
  235.7 4.2 %all-to-all-start.1 = ((bf16[128,4,2048]{2,0,1:T(8,128)(2,1)}), bf16[128,4,2048]{2,0,1:T(8,128)(2,1)S(1)}, u32[]{:S(2)}, u32[]{:S(2)}) async-start(bf16[128,4,2048]{2,0,1:T(8,128)(2,1)} %copy.20), calls=%async_computation.2 | async-start | bytes 4194304 | tf_op jit(solution)/shard_map/all_to_all | solution.py:118
  240.2 2.6 mul.119
  242.8 4.9 %mul.120 = f32[128,4,2048]{2,0,1:T(8,128)} reshape(f32[128,4,16,128]{3,2,0,1:T(8,128)} %mul.119) | data formatting | bytes 8388608 | tf_op jit(solution)/shard_map/mul | solution.py:124
  247.7 16.3 %all-to-all-done.1 = bf16[128,4,2048]{2,0,1:T(8,128)(2,1)S(1)} async-done(((bf16[128,4,2048]{2,0,1:T(8,128)(2,1)}), bf16[128,4,2048]{2,0,1:T(8,128)(2,1)S(1)}, u32[]{:S(2)}, u32[]{:S(2)}) %all-to-all-start.1) | async-done | bytes 2097184 | tf_op jit(solution)/shard_map/all_to_all | solution.py:118
  264.0 2.9 %multiply_reduce_fusion = f32[128,2048]{1,0:T(8,128)S(1)} fusion(f32[128,4,2048]{2,0,1:T(8,128)} %mul.120, bf16[128,4,2048]{2,0,1:T(8,128)(2,1)S(1)} %all-to-all-done.1), kind=kLoop, calls=%fused_computation.1 | loop fusion | flops 2883584 | bytes 7340032 | tf_op jit(solution)/shard_map/reduce_sum | solution.py:123
  267.2 1.2 fusion.16
  (34 shorter events, 6.9 us)
Async XLA Ops:
  7.2 52.3 %all-gather.7.cloned.1.call-start = ((), (), s32[]{:S(2)}) async-start(), calls=%async_computation.5 | async-start | bytes 4718592 | tf_op jit(solution)/shard_map/all_gather | solution.py:71
  7.9 94.4 %all-gather.5.cloned.1.call-start = ((), (), s32[]{:S(2)}) async-start(), calls=%async_computation.4 | async-start | bytes 2621440 | tf_op jit(solution)/shard_map/all_gather | solution.py:66
  8.6 143.5 %reduce-scatter.2.cloned.1.call-start = ((), (), s32[]{:S(2)}) async-start(), calls=%async_computation.6 | async-start | bytes 4718592 | tf_op jit(solution)/shard_map/reduce_scatter | solution.py:82
  101.3 0.7 copy-start.1
  101.3 102.1 %all-gather.9.cloned.1.call-start = ((), (), s32[]{:S(2)}) async-start(), calls=%async_computation.7 | async-start | bytes 2621440 | tf_op jit(solution)/shard_map/all_gather | solution.py:91
  203.4 2.8 %copy-start = (bf16[128,8,16,128]{3,2,1,0:T(8,128)(2,1)S(1)}, bf16[128,8,16,128]{3,2,1,0:T(8,128)(2,1)}, u32[]{:S(2)}) copy-start(bf16[128,8,16,128]{3,2,1,0:T(8,128)(2,1)} %param.16) | copy-start | bytes 12582916
  211.3 8.8 %all-to-all-start = ((f32[128,4,16]{0,2,1:T(8,128)}), f32[128,4,16]{0,2,1:T(8,128)S(1)}, u32[]{:S(2)}, u32[]{:S(2)}) async-start(f32[128,4,16]{0,2,1:T(8,128)} %bitcast.6), calls=%async_computation.1 | async-start | bytes 65536 | tf_op jit(solution)/shard_map/all_to_all | solution.py:111
  220.1 15.6 %all-to-all-start.2 = ((f32[128,4,16]{0,2,1:T(8,128)}), f32[128,4,16]{0,2,1:T(8,128)S(1)}, u32[]{:S(2)}, u32[]{:S(2)}) async-start(f32[128,4,16]{0,2,1:T(8,128)} %bitcast.7), calls=%async_computation.3 | async-start | bytes 65536 | tf_op jit(solution)/shard_map/all_to_all | solution.py:114
  235.7 28.2 %all-to-all-start.1 = ((bf16[128,4,2048]{2,0,1:T(8,128)(2,1)}), bf16[128,4,2048]{2,0,1:T(8,128)(2,1)S(1)}, u32[]{:S(2)}, u32[]{:S(2)}) async-start(bf16[128,4,2048]{2,0,1:T(8,128)(2,1)} %copy.20), calls=%async_computation.2 | async-start | bytes 4194304 | tf_op jit(solution)/shard_map/all_to_all | solution.py:118
Sparse Core Ops, SparseCore 0:
  9.6 49.8 all-gather.6
  61.3 38.7 all-gather.4
  102.4 49.6 reduce-scatter.1
  169.9 33.4 all-gather.8
where the time goes:
time: 276 us; the launch traced here: 275 us
  waiting for transfers between devices  137 us (50%)
  matrix products  42.2 us (15%)
  blocking collectives  38.9 us (14%)
  local copies, waits for them, and re-layouts  19 us (7%)
  between operations  13.9 us (5%)
  starting transfers between devices  11.9 us (4%)
  other arithmetic  11.7 us (4%)
    reduce_scatter x1, waiting for transfers between devices, per_device(): lax.psum_scatter(lowrank_change.astype(jnp.float32).astype(jnp.bfloat16),...  49.9 us
    all_gather x1, waiting for transfers between devices, per_device(): lax.all_gather(tokens, 'ad', axis=0, tiled=True)  36.2 us
    all_gather x1, waiting for transfers between devices, per_device(): every_head = lax.all_gather(queries, 'tp', axis=1, tiled=True)  33.5 us
    psum x1, blocking collectives, per_device(): reduced_rows = lax.psum(partial_value_sum, 'tp').astype(jnp.bfloat16)  25.3 us
    all_to_all x1, waiting for transfers between devices, per_device(): lax.all_to_all(partial_out.reshape(rows, tp_count, -1), 'tp', split_axis=...  16.3 us
    dot_general x1, matrix products, per_device(): jnp.dot(lax.all_gather(tokens, 'tp', axis=1, tiled=True), query_weight, p...  15.7 us
    all_gather x1, blocking collectives, per_device(): lax.all_gather(row_adapter_index, 'ad', axis=0, tiled=True)  13.5 us
    dot_general x1, matrix products, expand_rows(): jnp.einsum('pow,owu->pu', spread_rows, adapter_up_weight, preferred_eleme...  8.29 us
  transfers between devices with their start and end apart: 7, of which 4 were waited for; matrix products, arithmetic and copies ran while one was open for 15% of the time, Pallas kernels for 0%

commit v1 on v0

--- a/solution.py
+++ b/solution.py
@@ -1,9 +1,572 @@
+import functools
 import math
 
 import jax
 import jax.numpy as jnp
 from jax import lax
+from jax.experimental import pallas as pl
+from jax.experimental.pallas import tpu as pltpu
 from jax.sharding import PartitionSpec as P
+
+MESH = pl.DeviceIdType.MESH
+LANES = 128
+
+
+def remote(src, dst, send_sem, recv_sem, axis, peer):
+    return pltpu.make_async_remote_copy(
+        src_ref=src,
+        dst_ref=dst,
+        send_sem=send_sem,
+        recv_sem=recv_sem,
+        device_id={axis: peer},
+        device_id_type=MESH,
+    )
+
+
+def greet(counts):
+    barrier = pltpu.get_barrier_semaphore()
+    total = 0
+    for axis, count in counts:
+        me = lax.axis_index(axis)
+        for d in range(1, count):
+            pl.semaphore_signal(
+                barrier, inc=1, device_id={axis: lax.rem(me + d, count)}, device_id_type=MESH
+            )
+            total += 1
+    pl.semaphore_wait(barrier, total)
+
+
+def query_kernel(
+    n_ad,
+    n_tp,
+    cap,
+    rank,
+    packed_ref,
+    unpack_ref,
+    tokens_ref,
+    cos_ref,
+    sin_ref,
+    weight_hbm,
+    down_hbm,
+    up_hbm,
+    out_ref,
+    gathered,
+    arrived,
+    outgoing,
+    returned,
+    part_send,
+    part_recv,
+    acc,
+    weight_buf,
+    down_buf,
+    down_wide,
+    up_buf,
+    weight_sem,
+    down_sem,
+    up_sem,
+    tok_send,
+    tok_recv,
+    row_send,
+    row_recv,
+    sum_send,
+    sum_recv,
+    ret_send,
+    ret_recv,
+):
+    ad = lax.axis_index("ad")
+    tp = lax.axis_index("tp")
+    features = tokens_ref.shape[1]
+    columns = out_ref.shape[1]
+    depth = weight_buf.shape[1]
+    slots = weight_buf.shape[0]
+    subs = features // depth
+    steps = n_tp * subs
+    per = LANES // rank
+    wide = down_wide.shape[2]
+    tiles = down_wide.shape[0]
+    groups = n_ad // 2
+    rows2 = 2 * cap
+
+    def weight_copy(i):
+        owner = lax.rem(tp + n_tp - i // subs, n_tp)
+        start = pl.multiple_of(owner * features + (i % subs) * depth, depth)
+        return pltpu.make_async_copy(
+            weight_hbm.at[pl.ds(start, depth), :], weight_buf.at[i % slots], weight_sem.at[i % slots]
+        )
+
+    pairs = down_buf.shape[0] // 2
+    down_copies = [
+        pltpu.make_async_copy(
+            down_hbm.at[pl.ds(2 * j, 2)], down_buf.at[pl.ds(2 * j, 2)], down_sem.at[j]
+        )
+        for j in range(pairs)
+    ]
+    for copy in down_copies:
+        copy.start()
+    for i in range(slots):
+        weight_copy(i).start()
+    up_copy = pltpu.make_async_copy(up_hbm, up_buf, up_sem)
+    up_copy.start()
+
+    greet((("ad", n_ad), ("tp", n_tp)))
+
+    row_copies = []
+    for d in range(1, n_ad):
+        peer = lax.rem(ad + d, n_ad)
+        copy = remote(
+            packed_ref.at[peer], arrived.at[d], row_send.at[d], row_recv.at[d], "ad", peer
+        )
+        copy.start()
+        row_copies.append(copy)
+    tok_copies = []
+    for e in range(1, n_tp):
+        copy = remote(
+            tokens_ref, gathered.at[e], tok_send.at[e], tok_recv.at[e], "tp", lax.rem(tp + e, n_tp)
+        )
+        copy.start()
+        tok_copies.append(copy)
+    arrived[0] = packed_ref[ad]
+
+    per_tile = wide // LANES
+    for j in range(pairs):
+        down_copies[j].wait()
+
+        @pl.loop(0, features // 256)
+        def _(c):
+            at = pl.ds(pl.multiple_of(c * 256, 256), 256)
+            down_wide[j // per_tile, at, pl.ds((j % per_tile) * LANES, LANES)] = jnp.concatenate(
+                [down_buf[2 * j, at, :], down_buf[2 * j + 1, at, :]], axis=1
+            )
+
+    def base_chunk(e):
+        if e:
+            tok_copies[e - 1].wait_recv()
+        block = tokens_ref if e == 0 else gathered.at[e]
+        for sub in range(subs):
+            i = e * subs + sub
+            weight_copy(i).wait()
+
+            @pl.loop(0, columns // 256)
+            def _(c):
+                at = pl.ds(pl.multiple_of(c * 256, 256), 256)
+                product = jnp.dot(
+                    block[:, pl.ds(sub * depth, depth)],
+                    weight_buf[i % slots, :, at],
+                    preferred_element_type=jnp.float32,
+                )
+                if i == 0:
+                    acc[:, at] = product
+                else:
+                    acc[:, at] += product
+
+            if i + slots < steps:
+                weight_copy(i + slots).start()
+
+    lane2 = lax.broadcasted_iota(jnp.int32, (rows2, LANES), 1)
+    part_of = (lane2 // rank).astype(jnp.float32)
+    lane1 = lax.broadcasted_iota(jnp.int32, (cap, LANES), 1)
+    sum_copies = {}
+    ret_copies = []
+
+    def ids_of(g):
+        return (
+            arrived[pl.ds(2 * g, 2), :, pl.ds(features, LANES)]
+            .reshape(rows2, LANES)
+            .astype(jnp.float32)
+            - 1.0
+        )
+
+    def shrink(g):
+        for d in (2 * g, 2 * g + 1):
+            if d:
+                row_copies[d - 1].wait_recv()
+        ids = ids_of(g) - part_of
+
+        def tile(t, total):
+            product = jnp.dot(
+                arrived[pl.ds(2 * g, 2), :, pl.ds(0, features)].reshape(rows2, features),
+                down_wide[t],
+                preferred_element_type=jnp.float32,
+            )
+            for k in range(per_tile):
+                want = ((t * per_tile + k) * per).astype(jnp.float32)
+                total = total + jnp.where(
+                    ids == want, product[:, k * LANES : (k + 1) * LANES], 0.0
+                )
+            return total
+
+        total = lax.fori_loop(0, tiles, tile, jnp.zeros((rows2, LANES), jnp.float32))
+        total = total + pltpu.roll(total, rank, 1)
+        part_send[g] = jnp.where(lane1 < rank, total[:cap], total[cap:])
+        for e in range(1, n_tp):
+            copy = remote(
+                part_send.at[g],
+                part_recv.at[g, e],
+                sum_send.at[g, e],
+                sum_recv.at[g, e],
+                "tp",
+                lax.rem(tp + e, n_tp),
+            )
+            copy.start()
+            sum_copies[g, e] = copy
+
+    def expand(g):
+        if g == 0:
+            up_copy.wait()
+        total = part_send[g]
+        for e in range(1, n_tp):
+            sum_copies[g, e].wait_recv()
+            total = total + part_recv[g, e]
+        turned = pltpu.roll(total, rank, 1)
+        both = jnp.concatenate(
+            [jnp.where(lane1 < rank, total, turned), jnp.where(lane1 < rank, turned, total)], axis=0
+        )
+        ids = ids_of(g) - part_of
+        spread = jnp.concatenate(
+            [jnp.where(ids == float(j * per), both, 0.0).astype(jnp.bfloat16) for j in range(pairs)],
+            axis=1,
+        )
+
+        @pl.loop(0, columns // 256)
+        def _(c):
+            at = pl.ds(pl.multiple_of(c * 256, 256), 256)
+            change = jnp.dot(spread, up_buf[:, at], preferred_element_type=jnp.float32)
+            outgoing[pl.ds(2 * g, 2), :, at] = change.astype(jnp.bfloat16).reshape(2, cap, 256)
+
+        for d in (2 * g, 2 * g + 1):
+            if d:
+                copy = remote(
+                    outgoing.at[d],
+                    returned.at[ad],
+                    ret_send.at[d],
+                    ret_recv.at[d],
+                    "ad",
+                    lax.rem(ad + n_ad - d, n_ad),
+                )
+                copy.start()
+                ret_copies.append(copy)
+            else:
+                returned[ad] = outgoing[0]
+
+    shrink(0)
+    base_chunk(0)
+    expand(0)
+    for g in range(1, groups):
+        shrink(g)
+        if g < n_tp:
+            base_chunk(g)
+        expand(g)
+    for e in range(groups, n_tp):
+        base_chunk(e)
+    for copy in ret_copies:
+        copy.wait_recv()
+
+    head = cos_ref.shape[1]
+
+    @pl.loop(0, columns // 256)
+    def _(c):
+        at = pl.ds(pl.multiple_of(c * 256, 256), 256)
+        delta = jnp.dot(
+            unpack_ref[...],
+            returned[:, :, at].reshape(n_ad * cap, 256),
+            preferred_element_type=jnp.float32,
+        )
+        query = acc[:, at] + delta
+        pieces = []
+        for h in range(256 // head):
+            one = query[:, h * head : (h + 1) * head]
+            pieces.append(one * cos_ref[...] + pltpu.roll(one, head // 2, 1) * sin_ref[...])
+        out_ref[:, at] = jnp.concatenate(pieces, axis=1).astype(jnp.bfloat16)
+
+    for copy in row_copies + tok_copies + list(sum_copies.values()) + ret_copies:
+        copy.wait_send()
+
+
+def attend_kernel(
+    n_tp,
+    chunk,
+    span,
+    kv_heads,
+    lengths_ref,
+    queries_ref,
+    keys_hbm,
+    values_hbm,
+    out_ref,
+    every,
+    keys,
+    values,
+    part,
+    stat,
+    part_in,
+    stat_in,
+    key_sem,
+    value_sem,
+    q_send,
+    q_recv,
+    p_send,
+    p_recv,
+    s_send,
+    s_recv,
+):
+    tp = lax.axis_index("tp")
+    rows, heads, size = queries_ref.shape
+    chunks = rows // chunk
+    all_heads = n_tp * heads
+    cells = kv_heads * span
+    scale = 1.0 / math.sqrt(size)
+    loads = []
+    for c in range(chunks):
+        at = pl.ds(c * chunk, chunk)
+        pair = (
+            pltpu.make_async_copy(keys_hbm.at[at], keys.at[at], key_sem.at[c]),
+            pltpu.make_async_copy(values_hbm.at[at], values.at[at], value_sem.at[c]),
+        )
+        for copy in pair:
+            copy.start()
+        loads.append(pair)
+    greet((("tp", n_tp),))
+    sends = {}
+    for c in range(chunks):
+        at = pl.ds(c * chunk, chunk)
+        for e in range(1, n_tp):
+            copy = remote(
+                queries_ref.at[at],
+                every.at[tp, at],
+                q_send.at[c, e],
+                q_recv.at[c, e],
+                "tp",
+                lax.rem(tp + e, n_tp),
+            )
+            copy.start()
+            sends[c, e] = copy
+    every[tp] = queries_ref[...]
+
+    head_of = lax.broadcasted_iota(jnp.int32, (all_heads, cells), 0) // (all_heads // kv_heads)
+    cell = lax.broadcasted_iota(jnp.int32, (all_heads, cells), 1)
+    mine = head_of == cell // span
+    position = jnp.where(mine, tp * span + cell % span, 1 << 30)
+    lane = lax.broadcasted_iota(jnp.int32, (all_heads, LANES), 1)
+    lane_h = lax.broadcasted_iota(jnp.int32, (heads, LANES), 1)
+    unroll = 4
+    outs = []
+
+    def attend(c):
+        for copy in loads[c]:
+            copy.wait()
+        for e in range(1, n_tp):
+            sends[c, e].wait_recv()
+
+        def some(b, held):
+            for u in range(unroll):
+                local = b * unroll + u
+                r = c * chunk + local
+                query = jnp.concatenate([every[t, r] for t in range(n_tp)], axis=0)
+                score = (
+                    lax.dot_general(
+                        query, keys[r], (((1,), (1,)), ((), ())), preferred_element_type=jnp.float32
+                    )
+                    * scale
+                )
+                valid = position < lengths_ref[r]
+                score = jnp.where(valid, score, -1e30)
+                peak = jnp.max(score, axis=1, keepdims=True)
+                weight = jnp.where(valid, jnp.exp(score - peak), 0.0)
+                total = jnp.sum(weight, axis=1, keepdims=True)
+                result = jnp.dot(
+                    weight.astype(jnp.bfloat16), values[r], preferred_element_type=jnp.float32
+                ).astype(jnp.bfloat16)
+                for t in range(n_tp):
+                    part[t, r] = result[t * heads : (t + 1) * heads]
+                held = jnp.where(lane == local, peak, held)
+                held = jnp.where(lane == local + LANES // 2, total, held)
+            return held
+
+        held = lax.fori_loop(
+            0, chunk // unroll, some, jnp.zeros((all_heads, LANES), jnp.float32)
+        )
+        for t in range(n_tp):
+            stat[c, t] = held[t * heads : (t + 1) * heads]
+        at = pl.ds(c * chunk, chunk)
+        for e in range(1, n_tp):
+            peer = lax.rem(tp + e, n_tp)
+            p = remote(
+                part.at[peer, at], part_in.at[e, at], p_send.at[c, e], p_recv.at[c, e], "tp", peer
+            )
+            s = remote(
+                stat.at[c, peer], stat_in.at[c, e], s_send.at[c, e], s_recv.at[c, e], "tp", peer
+            )
+            s.start()
+            p.start()
+            outs.append((c, s))
+            outs.append((c, p))
+        part_in[0, at] = part[tp, at]
+        stat_in[c, 0] = stat[c, tp]
+
+    def combine(c):
+        for k, copy in outs:
+            if k == c:
+                copy.wait_recv()
+        stats = [stat_in[c, e] for e in range(n_tp)]
+        top = functools.reduce(jnp.maximum, stats)
+        factors = [jnp.exp(s - top) for s in stats]
+        denom = sum(f * pltpu.roll(s, LANES // 2, 1) for f, s in zip(factors, stats))
+        shares = [f / denom for f in factors]
+
+        @pl.loop(0, chunk // unroll)
+        def _(b):
+            for u in range(unroll):
+                local = b * unroll + u
+                r = c * chunk + local
+                result = jnp.zeros((heads, size), jnp.float32)
+                for e in range(n_tp):
+                    share = jnp.sum(
+                        jnp.where(lane_h == local, shares[e], 0.0), axis=1, keepdims=True
+                    )
+                    result = result + share * part_in[e, r].astype(jnp.float32)
+                out_ref[r] = result.astype(jnp.bfloat16)
+
+    for c in range(chunks):
+        attend(c)
+        if c:
+            combine(c - 1)
+    combine(chunks - 1)
+    for copy in list(sends.values()) + [copy for _, copy in outs]:
+        copy.wait_send()
+
+
+def fused_device(
+    tokens,
+    query_weight,
+    adapter_down_weight,
+    adapter_up_weight,
+    row_adapter_index,
+    adapter_table_slot,
+    lengths,
+    cached_key_rows,
+    cached_value_rows,
+):
+    rows, features = tokens.shape
+    columns = query_weight.shape[1]
+    n_ad = lax.axis_size("ad")
+    n_tp = lax.axis_size("tp")
+    held = adapter_down_weight.shape[0]
+    rank = adapter_down_weight.shape[2]
+    _, kv_heads, span, head_dim = cached_key_rows.shape
+    cap = -(-(384 // n_ad) // 16) * 16
+
+    slots = lookup(row_adapter_index, adapter_table_slot)
+    owner = slots // held
+    order = jnp.arange(rows, dtype=jnp.int32)
+    before = (owner[:, None] == owner[None, :]) & (order[None, :] < order[:, None])
+    place = owner * cap + jnp.sum(before.astype(jnp.int32), axis=1)
+    cells = jnp.arange(n_ad * cap, dtype=jnp.int32)
+    pack = (cells[:, None] == place[None, :]).astype(jnp.bfloat16)
+    unpack = (place[:, None] == cells[None, :]).astype(jnp.bfloat16)
+    marked = jnp.concatenate(
+        [
+            tokens,
+            jnp.broadcast_to((slots % held + 1).astype(jnp.bfloat16)[:, None], (rows, LANES)),
+        ],
+        axis=1,
+    )
+    packed = jnp.dot(pack, marked, preferred_element_type=jnp.float32).astype(jnp.bfloat16)
+    packed = packed.reshape(n_ad, cap, features + LANES)
+
+    half = head_dim // 2
+    freq = jnp.exp(jnp.arange(half, dtype=jnp.float32) * (-2.0 * math.log(500000.0) / head_dim))
+    angle = (lengths - 1).astype(jnp.float32)[:, None] * freq[None, :]
+    cosine = jnp.cos(angle)
+    sine = jnp.sin(angle)
+    cos_full = jnp.concatenate([cosine, cosine], axis=1)
+    sin_full = jnp.concatenate([-sine, sine], axis=1)
+
+    depth = 1024
+    slot_count = 4
+    vmem = pl.BlockSpec(memory_space=pltpu.VMEM)
+    anywhere = pl.BlockSpec(memory_space=pl.ANY)
+    bf16, f32 = jnp.bfloat16, jnp.float32
+    dma = pltpu.SemaphoreType.DMA
+    groups = n_ad // 2
+    queries = pl.pallas_call(
+        functools.partial(query_kernel, n_ad, n_tp, cap, rank),
+        out_shape=jax.ShapeDtypeStruct((rows, columns), bf16),
+        in_specs=[vmem] * 5 + [anywhere] * 3,
+        out_specs=vmem,
+        scratch_shapes=[
+            pltpu.VMEM((n_tp, rows, features), bf16),
+            pltpu.VMEM((n_ad, cap, features + LANES), bf16),
+            pltpu.VMEM((n_ad, cap, columns), bf16),
+            pltpu.VMEM((n_ad, cap, columns), bf16),
+            pltpu.VMEM((groups, cap, LANES), f32),
+            pltpu.VMEM((groups, n_tp, cap, LANES), f32),
+            pltpu.VMEM((rows, columns), f32),
+            pltpu.VMEM((slot_count, depth, columns), bf16),
+            pltpu.VMEM((held, features, rank), bf16),
+            pltpu.VMEM((held * rank // 256, features, 256), bf16),
+            pltpu.VMEM((held * rank, columns), bf16),
+            dma((slot_count,)),
+            dma((held // 2,)),
+            dma,
+            dma((n_tp,)),
+            dma((n_tp,)),
+            dma((n_ad,)),
+            dma((n_ad,)),
+            dma((groups, n_tp)),
+            dma((groups, n_tp)),
+            dma((n_ad,)),
+            dma((n_ad,)),
+        ],
+        compiler_params=pltpu.CompilerParams(
+            collective_id=0, has_side_effects=True, vmem_limit_bytes=60 * 1024 * 1024
+        ),
+        name="project",
+    )(
+        packed,
+        unpack,
+        tokens,
+        cos_full,
+        sin_full,
+        query_weight,
+        adapter_down_weight,
+        adapter_up_weight.reshape(held * rank, columns),
+    )
+
+    heads = columns // head_dim
+    chunk = 32
+    chunks = rows // chunk
+    attended = pl.pallas_call(
+        functools.partial(attend_kernel, n_tp, chunk, span, kv_heads),
+        out_shape=jax.ShapeDtypeStruct((rows, heads, head_dim), bf16),
+        in_specs=[pl.BlockSpec(memory_space=pltpu.SMEM), vmem] + [anywhere] * 2,
+        out_specs=vmem,
+        scratch_shapes=[
+            pltpu.VMEM((n_tp, rows, heads, head_dim), bf16),
+            pltpu.VMEM((rows, kv_heads * span, head_dim), bf16),
+            pltpu.VMEM((rows, kv_heads * span, head_dim), bf16),
+            pltpu.VMEM((n_tp, rows, heads, head_dim), bf16),
+            pltpu.VMEM((chunks, n_tp, heads, LANES), f32),
+            pltpu.VMEM((n_tp, rows, heads, head_dim), bf16),
+            pltpu.VMEM((chunks, n_tp, heads, LANES), f32),
+            dma((chunks,)),
+            dma((chunks,)),
+            dma((chunks, n_tp)),
+            dma((chunks, n_tp)),
+            dma((chunks, n_tp)),
+            dma((chunks, n_tp)),
+            dma((chunks, n_tp)),
+            dma((chunks, n_tp)),
+        ],
+        compiler_params=pltpu.CompilerParams(
+            collective_id=1, has_side_effects=True, vmem_limit_bytes=48 * 1024 * 1024
+        ),
+        name="attend",
+    )(
+        lengths,
+        queries.reshape(rows, heads, head_dim),
+        cached_key_rows.reshape(rows, kv_heads * span, head_dim),
+        cached_value_rows.reshape(rows, kv_heads * span, head_dim),
+    )
+    return (queries, attended.reshape(rows, columns))
 
 
 def rotate(query, lengths):
@@ -130,8 +693,9 @@
 
 
 def solution(mesh):
+    fits = mesh.shape["tp"] <= 4 and mesh.shape["ad"] % 2 == 0
     return jax.shard_map(
-        per_device,
+        fused_device if fits else per_device,
         mesh=mesh,
         in_specs=(
             P("ad", "tp"),

time: 276 us -> 169 us (0.61)
  Pallas kernels: 0 us -> 148 us
  waiting for transfers between devices: 137 us -> 0 us
  matrix products: 42.2 us -> 2.9 us
  blocking collectives: 38.9 us -> 0 us
  between operations: 13.9 us -> 0.71 us
  starting transfers between devices: 11.9 us -> 0 us
  other arithmetic: 11.7 us -> 3.5 us
  local copies, waits for them, and re-layouts: 19 us -> 13.5 us
    pallas_call x0 -> x2, Pallas kernels: none -> 148 us  [the longest x1 87.4 us: fused_device(): pl.pallas_call(functools.partial(query_kernel, n_ad, n_tp, cap, rank), ou...]
    all_gather x3 -> x0, waiting for transfers between devices: 69.7 us -> none  [the longest x1 36.2 us: per_device(): lax.all_gather(tokens, 'ad', axis=0, tiled=True)]
    reduce_scatter x1 -> x0, waiting for transfers between devices: 49.9 us -> none  [per_device(): lax.psum_scatter(lowrank_change.astype(jnp.float32).astype(jnp.bfloat16),...]
    dot_general x4 -> x1, matrix products: 34.6 us -> 2.9 us  [fused_device(): jnp.dot(pack, marked, preferred_element_type=jnp.float32)]
    psum x1 -> x0, blocking collectives: 25.3 us -> none  [per_device(): reduced_rows = lax.psum(partial_value_sum, 'tp').astype(jnp.bfloat16)]
    all_to_all x3 -> x0, waiting for transfers between devices: 16.3 us -> none  [the longest x1 16.3 us: per_device(): lax.all_to_all(partial_out.reshape(rows, tp_count, -1), 'tp', split_axis=...]
    all_gather x1 -> x0, blocking collectives: 13.5 us -> none  [per_device(): lax.all_gather(row_adapter_index, 'ad', axis=0, tiled=True)]
    all_to_all x3 -> x0, starting transfers between devices: 11.6 us -> none  [the longest x1 4.19 us: per_device(): lax.all_to_all(partial_out.reshape(rows, tp_count, -1), 'tp', split_axis=...]
  transfers between devices with their start and end apart: 7 -> 0, of which waited for: 4 -> 0; matrix products, arithmetic and copies ran while one was open for 15% -> 0% of each run, Pallas kernels for 0% -> 0%
where the time goes in v1:
time: 169 us
  Pallas kernels  148 us (88%)
  local copies, waits for them, and re-layouts  13.5 us (8%)
  other arithmetic  3.5 us (2%)
  matrix products  2.9 us (2%)
    pallas_call x1, Pallas kernels, fused_device(): pl.pallas_call(functools.partial(query_kernel, n_ad, n_tp, cap, rank), ou...  87.4 us
    pallas_call x1, Pallas kernels, fused_device(): pl.pallas_call(functools.partial(attend_kernel, n_tp, chunk, span, kv_hea...  60.8 us
    unnamed x10, local copies, waits for them, and re-layouts  13.4 us

profile of v1, /device:TPU:0, one launch (start us, length us, event | category | flops | bytes accessed | tf_op | source)
XLA Modules:
  0.0 168.8 jit_solution(16897491273096632104)
XLA Ops:
  0.6 0.8 select_reduce_fusion
  1.5 0.7 add_convert_fusion
  2.2 0.2 convert_reduce_fusion
  2.4 0.1 broadcast_in_dim.16
  2.4 0.7 fusion.3.unpack_ref
  3.2 0.3 fusion.6
  3.5 0.8 pad_maximum_fusion
  4.3 2.9 %convolution_convert_fusion = bf16[384,2176]{1,0:T(8,128)(2,1)} fusion(bf16[128,128]{1,0:T(8,128)(2,1)S(1)} %broadcast_in_dim.16, bf16[128,2048]{1,0:T(8,128)(2,1)} %tokens_ref.1, s32[128]{0:T(128)S(1)} %multiply_add_fusion), kind=kOutput, calls=%fused_computation | convolution fusion | flops 215908352 | bytes 2228736 | tf_op jit(solution)/shard_map/dot_general | solution.py:472
  7.2 8.4 %copy.12.down_hbm = bf16[16,2048,64]{2,1,0:T(8,128)(2,1)} copy(bf16[16,2048,64]{1,2,0:T(8,128)(2,1)} %param.11) | data formatting | bytes 8388608 | tf_op args[2]
  15.5 0.0 copy-start.1
  15.5 87.4 %project.1 = bf16[128,2048]{1,0:T(8,128)(2,1)} custom-call(bf16[8,48,2176]{2,1,0:T(8,128)(2,1)} %bitcast.13, bf16[128,384]{1,0:T(8,128)(2,1)} %fusion.3.unpack_ref, bf16[128,2048]{1,0:T(8,128)(2,1)} %tokens_ref.1, f32[128,128]{1,0:T(8,128)} %get-tuple-element.7.cos_ref, f32[128,128]{1,0:T(8,128)} %get-tuple-element.8.sin_ref, bf16[8192,2048]{1,0:T(8,128)(2,1)} %weight_hbm.1, ...), custom_call_target="tpu_custom_call" | custom-call | tf_op jit(solution)/shard_map/project/pallas_call | solution.py:490
  103.0 1.1 copy.13
  104.1 0.0 copy-done.1
  104.2 0.0 copy-start
  104.2 2.2 %copy-done = bf16[128,8,16,128]{3,2,1,0:T(8,128)(2,1)S(1)} copy-done((bf16[128,8,16,128]{3,2,1,0:T(8,128)(2,1)S(1)}, bf16[128,8,16,128]{3,2,1,0:T(8,128)(2,1)}, u32[]{:S(2)}) %copy-start) | copy-done | bytes 4194328
  106.3 0.0 copy-start.2
  106.3 60.8 %attend.1 = bf16[128,16,128]{2,1,0:T(8,128)(2,1)S(1)} custom-call(s32[128]{0:T(128)S(1)} %copy-done.1, bf16[128,16,128]{2,1,0:T(8,128)(2,1)S(1)} %bitcast.12, bf16[128,128,128]{2,1,0:T(8,128)(2,1)S(1)} %bitcast.10, bf16[128,128,128]{2,1,0:T(8,128)(2,1)} %bitcast.16), custom_call_target="tpu_custom_call" | custom-call | tf_op jit(solution)/shard_map/attend/pallas_call | solution.py:537
  167.1 0.9 copy.16
  168.0 0.0 copy-done.2
  168.0 0.8 copy.18
  (3 shorter events, 0.0 us)
Async XLA Ops:
  15.5 88.6 %copy-start.1 = (s32[128]{0:T(128)S(1)}, s32[128]{0:T(128)}, u32[]{:S(2)}) copy-start(s32[128]{0:T(128)} %lengths_ref.1) | copy-start | bytes 1540
  104.2 2.2 %copy-start = (bf16[128,8,16,128]{3,2,1,0:T(8,128)(2,1)S(1)}, bf16[128,8,16,128]{3,2,1,0:T(8,128)(2,1)}, u32[]{:S(2)}) copy-start(bf16[128,8,16,128]{3,2,1,0:T(8,128)(2,1)} %param.16) | copy-start | bytes 12582916
  106.3 61.7 %copy-start.2 = (bf16[128,2048]{1,0:T(8,128)(2,1)S(1)}, bf16[128,2048]{1,0:T(8,128)(2,1)}, u32[]{:S(2)}) copy-start(bf16[128,2048]{1,0:T(8,128)(2,1)} %project.1) | copy-start | bytes 1572868

commit v2 on v1

--- a/solution.py
+++ b/solution.py
@@ -10,6 +10,7 @@
 
 MESH = pl.DeviceIdType.MESH
 LANES = 128
+SWAPPED = 64
 
 
 def remote(src, dst, send_sem, recv_sem, axis, peer):
@@ -36,20 +37,28 @@
     pl.semaphore_wait(barrier, total)
 
 
-def query_kernel(
+def step_kernel(
     n_ad,
     n_tp,
     cap,
     rank,
-    packed_ref,
+    swapped,
+    chunk,
+    place_ref,
+    mark_ref,
     unpack_ref,
     tokens_ref,
     cos_ref,
     sin_ref,
+    lengths_ref,
     weight_hbm,
     down_hbm,
     up_hbm,
+    keys_hbm,
+    values_hbm,
     out_ref,
+    att_ref,
+    packed,
     gathered,
     arrived,
     outgoing,
@@ -59,11 +68,20 @@
     acc,
     weight_buf,
     down_buf,
-    down_wide,
     up_buf,
+    heads_f32,
+    heads_bf16,
+    swap_keys,
+    swap_values,
+    every,
+    keys,
+    values,
+    part,
+    stat,
+    part_in,
+    stat_in,
     weight_sem,
-    down_sem,
-    up_sem,
+    load_sem,
     tok_send,
     tok_recv,
     row_send,
@@ -72,20 +90,37 @@
     sum_recv,
     ret_send,
     ret_recv,
+    swap_send,
+    swap_recv,
+    q_send,
+    q_recv,
+    p_send,
+    p_recv,
+    s_send,
+    s_recv,
 ):
     ad = lax.axis_index("ad")
     tp = lax.axis_index("tp")
-    features = tokens_ref.shape[1]
+    rows, features = tokens_ref.shape
     columns = out_ref.shape[1]
     depth = weight_buf.shape[1]
     slots = weight_buf.shape[0]
     subs = features // depth
     steps = n_tp * subs
     per = LANES // rank
-    wide = down_wide.shape[2]
-    tiles = down_wide.shape[0]
+    pairs = down_buf.shape[0] // LANES
+    tiles = down_buf.shape[0] // 256
+    per_tile = 256 // LANES
     groups = n_ad // 2
     rows2 = 2 * cap
+    heads, size = heads_bf16.shape[1:]
+    kv_heads, span = keys_hbm.shape[1:3]
+    kv_mine = kv_heads // n_tp
+    spread_rows = rows - swapped
+    chunks = spread_rows // chunk
+    all_heads = n_tp * heads
+    cells = kv_heads * span
+    scale = 1.0 / math.sqrt(size)
 
     def weight_copy(i):
         owner = lax.rem(tp + n_tp - i // subs, n_tp)
@@ -94,30 +129,24 @@
             weight_hbm.at[pl.ds(start, depth), :], weight_buf.at[i % slots], weight_sem.at[i % slots]
         )
 
-    pairs = down_buf.shape[0] // 2
-    down_copies = [
-        pltpu.make_async_copy(
-            down_hbm.at[pl.ds(2 * j, 2)], down_buf.at[pl.ds(2 * j, 2)], down_sem.at[j]
-        )
-        for j in range(pairs)
-    ]
-    for copy in down_copies:
-        copy.start()
+    down_copy = pltpu.make_async_copy(down_hbm, down_buf, load_sem.at[0])
+    up_copy = pltpu.make_async_copy(up_hbm, up_buf, load_sem.at[1])
+    down_copy.start()
     for i in range(slots):
         weight_copy(i).start()
-    up_copy = pltpu.make_async_copy(up_hbm, up_buf, up_sem)
     up_copy.start()
+    early = pl.ds(0, swapped)
+    late = pl.ds(swapped, spread_rows)
+    own_kv = pl.ds(tp * kv_mine, kv_mine)
+    cache_copies = [
+        pltpu.make_async_copy(keys_hbm.at[early, own_kv], swap_keys.at[:, 0], load_sem.at[2]),
+        pltpu.make_async_copy(values_hbm.at[early, own_kv], swap_values.at[:, 0], load_sem.at[3]),
+        pltpu.make_async_copy(keys_hbm.at[late], keys, load_sem.at[4]),
+        pltpu.make_async_copy(values_hbm.at[late], values, load_sem.at[5]),
+    ]
 
     greet((("ad", n_ad), ("tp", n_tp)))
 
-    row_copies = []
-    for d in range(1, n_ad):
-        peer = lax.rem(ad + d, n_ad)
-        copy = remote(
-            packed_ref.at[peer], arrived.at[d], row_send.at[d], row_recv.at[d], "ad", peer
-        )
-        copy.start()
-        row_copies.append(copy)
     tok_copies = []
     for e in range(1, n_tp):
         copy = remote(
@@ -125,18 +154,47 @@
         )
         copy.start()
         tok_copies.append(copy)
-    arrived[0] = packed_ref[ad]
-
-    per_tile = wide // LANES
-    for j in range(pairs):
-        down_copies[j].wait()
-
-        @pl.loop(0, features // 256)
+
+    cell_row = lax.broadcasted_iota(jnp.int32, (cap, rows), 0)
+
+    def pack_into(d, peer, target):
+        pick = (cell_row + peer * cap == place_ref[...]).astype(jnp.bfloat16)
+
+        @pl.loop(0, features // 512)
         def _(c):
-            at = pl.ds(pl.multiple_of(c * 256, 256), 256)
-            down_wide[j // per_tile, at, pl.ds((j % per_tile) * LANES, LANES)] = jnp.concatenate(
-                [down_buf[2 * j, at, :], down_buf[2 * j + 1, at, :]], axis=1
-            )
+            at = pl.ds(pl.multiple_of(c * 512, 512), 512)
+            target[d, :, at] = jnp.dot(
+                pick, tokens_ref[:, at], preferred_element_type=jnp.float32
+            ).astype(jnp.bfloat16)
+
+        target[d, :, pl.ds(features, LANES)] = jnp.dot(
+            pick, mark_ref[...], preferred_element_type=jnp.float32
+        ).astype(jnp.bfloat16)
+
+    row_copies = []
+    for d in range(1, n_ad):
+        peer = lax.rem(ad + d, n_ad)
+        pack_into(d, peer, packed)
+        copy = remote(packed.at[d], arrived.at[d], row_send.at[d], row_recv.at[d], "ad", peer)
+        copy.start()
+        row_copies.append(copy)
+    pack_into(0, ad, arrived)
+
+    swap_copies = []
+
+    def swap(which, source, target):
+        for e in range(1, n_tp):
+            peer = lax.rem(tp + e, n_tp)
+            copy = remote(
+                source.at[early, pl.ds(peer * kv_mine, kv_mine)],
+                target.at[:, e],
+                swap_send.at[which, e],
+                swap_recv.at[which, e],
+                "tp",
+                peer,
+            )
+            copy.start()
+            swap_copies.append(copy)
 
     def base_chunk(e):
         if e:
@@ -180,12 +238,15 @@
         for d in (2 * g, 2 * g + 1):
             if d:
                 row_copies[d - 1].wait_recv()
+        if g == 0:
+            down_copy.wait()
         ids = ids_of(g) - part_of
 
         def tile(t, total):
-            product = jnp.dot(
+            product = lax.dot_general(
                 arrived[pl.ds(2 * g, 2), :, pl.ds(0, features)].reshape(rows2, features),
-                down_wide[t],
+                down_buf[pl.ds(pl.multiple_of(t * 256, 256), 256), :],
+                (((1,), (1,)), ((), ())),
                 preferred_element_type=jnp.float32,
             )
             for k in range(per_tile):
@@ -248,20 +309,22 @@
             else:
                 returned[ad] = outgoing[0]
 
+    swap(0, keys_hbm, swap_keys)
     shrink(0)
     base_chunk(0)
     expand(0)
+    for copy in cache_copies:
+        copy.start()
     for g in range(1, groups):
         shrink(g)
         if g < n_tp:
             base_chunk(g)
         expand(g)
+    swap(1, values_hbm, swap_values)
     for e in range(groups, n_tp):
         base_chunk(e)
     for copy in ret_copies:
         copy.wait_recv()
-
-    head = cos_ref.shape[1]
 
     @pl.loop(0, columns // 256)
     def _(c):
@@ -273,65 +336,21 @@
         )
         query = acc[:, at] + delta
         pieces = []
-        for h in range(256 // head):
-            one = query[:, h * head : (h + 1) * head]
-            pieces.append(one * cos_ref[...] + pltpu.roll(one, head // 2, 1) * sin_ref[...])
+        for h in range(256 // size):
+            one = query[:, h * size : (h + 1) * size]
+            pieces.append(one * cos_ref[...] + pltpu.roll(one, size // 2, 1) * sin_ref[...])
         out_ref[:, at] = jnp.concatenate(pieces, axis=1).astype(jnp.bfloat16)
 
-    for copy in row_copies + tok_copies + list(sum_copies.values()) + ret_copies:
-        copy.wait_send()
-
-
-def attend_kernel(
-    n_tp,
-    chunk,
-    span,
-    kv_heads,
-    lengths_ref,
-    queries_ref,
-    keys_hbm,
-    values_hbm,
-    out_ref,
-    every,
-    keys,
-    values,
-    part,
-    stat,
-    part_in,
-    stat_in,
-    key_sem,
-    value_sem,
-    q_send,
-    q_recv,
-    p_send,
-    p_recv,
-    s_send,
-    s_recv,
-):
-    tp = lax.axis_index("tp")
-    rows, heads, size = queries_ref.shape
-    chunks = rows // chunk
-    all_heads = n_tp * heads
-    cells = kv_heads * span
-    scale = 1.0 / math.sqrt(size)
-    loads = []
-    for c in range(chunks):
-        at = pl.ds(c * chunk, chunk)
-        pair = (
-            pltpu.make_async_copy(keys_hbm.at[at], keys.at[at], key_sem.at[c]),
-            pltpu.make_async_copy(values_hbm.at[at], values.at[at], value_sem.at[c]),
-        )
-        for copy in pair:
-            copy.start()
-        loads.append(pair)
-    greet((("tp", n_tp),))
+    for h in range(heads):
+        heads_f32[:, h, :] = out_ref[:, h * size : (h + 1) * size].astype(jnp.float32)
+    heads_bf16[...] = heads_f32[...].astype(jnp.bfloat16)
+
     sends = {}
     for c in range(chunks):
-        at = pl.ds(c * chunk, chunk)
         for e in range(1, n_tp):
             copy = remote(
-                queries_ref.at[at],
-                every.at[tp, at],
+                heads_bf16.at[pl.ds(swapped + c * chunk, chunk)],
+                every.at[tp, pl.ds(c * chunk, chunk)],
                 q_send.at[c, e],
                 q_recv.at[c, e],
                 "tp",
@@ -339,7 +358,44 @@
             )
             copy.start()
             sends[c, e] = copy
-    every[tp] = queries_ref[...]
+    every[tp] = heads_bf16[pl.ds(swapped, spread_rows)]
+
+    for copy in swap_copies:
+        copy.wait_recv()
+    for copy in cache_copies:
+        copy.wait()
+
+    own_head = lax.broadcasted_iota(jnp.int32, (heads, cells), 0) // (heads // kv_mine)
+    own_cell = lax.broadcasted_iota(jnp.int32, (heads, cells), 1)
+    block = kv_mine * span
+    own_mine = own_head == (own_cell % block) // span
+    source = lax.rem(tp + n_tp - own_cell // block, n_tp)
+    own_position = jnp.where(own_mine, source * span + own_cell % span, 1 << 30)
+
+    @pl.loop(0, swapped // 8)
+    def _(b):
+        for u in range(8):
+            r = b * 8 + u
+            score = (
+                lax.dot_general(
+                    heads_bf16[r],
+                    swap_keys[r].reshape(cells, size),
+                    (((1,), (1,)), ((), ())),
+                    preferred_element_type=jnp.float32,
+                )
+                * scale
+            )
+            valid = own_position < lengths_ref[r]
+            score = jnp.where(valid, score, -1e30)
+            peak = jnp.max(score, axis=1, keepdims=True)
+            weight = jnp.where(valid, jnp.exp(score - peak), 0.0)
+            total = jnp.sum(weight, axis=1, keepdims=True)
+            result = jnp.dot(
+                weight.astype(jnp.bfloat16),
+                swap_values[r].reshape(cells, size),
+                preferred_element_type=jnp.float32,
+            )
+            heads_f32[r] = result / total
 
     head_of = lax.broadcasted_iota(jnp.int32, (all_heads, cells), 0) // (all_heads // kv_heads)
     cell = lax.broadcasted_iota(jnp.int32, (all_heads, cells), 1)
@@ -351,8 +407,6 @@
     outs = []
 
     def attend(c):
-        for copy in loads[c]:
-            copy.wait()
         for e in range(1, n_tp):
             sends[c, e].wait_recv()
 
@@ -363,17 +417,22 @@
                 query = jnp.concatenate([every[t, r] for t in range(n_tp)], axis=0)
                 score = (
                     lax.dot_general(
-                        query, keys[r], (((1,), (1,)), ((), ())), preferred_element_type=jnp.float32
+                        query,
+                        keys[r].reshape(cells, size),
+                        (((1,), (1,)), ((), ())),
+                        preferred_element_type=jnp.float32,
                     )
                     * scale
                 )
-                valid = position < lengths_ref[r]
+                valid = position < lengths_ref[swapped + r]
                 score = jnp.where(valid, score, -1e30)
                 peak = jnp.max(score, axis=1, keepdims=True)
                 weight = jnp.where(valid, jnp.exp(score - peak), 0.0)
                 total = jnp.sum(weight, axis=1, keepdims=True)
                 result = jnp.dot(
-                    weight.astype(jnp.bfloat16), values[r], preferred_element_type=jnp.float32
+                    weight.astype(jnp.bfloat16),
+                    values[r].reshape(cells, size),
+                    preferred_element_type=jnp.float32,
                 ).astype(jnp.bfloat16)
                 for t in range(n_tp):
                     part[t, r] = result[t * heads : (t + 1) * heads]
@@ -389,11 +448,11 @@
         at = pl.ds(c * chunk, chunk)
         for e in range(1, n_tp):
             peer = lax.rem(tp + e, n_tp)
+            s = remote(
+                stat.at[c, peer], stat_in.at[c, e], s_send.at[c, e], s_recv.at[c, e], "tp", peer
+            )
             p = remote(
                 part.at[peer, at], part_in.at[e, at], p_send.at[c, e], p_recv.at[c, e], "tp", peer
-            )
-            s = remote(
-                stat.at[c, peer], stat_in.at[c, e], s_send.at[c, e], s_recv.at[c, e], "tp", peer
             )
             s.start()
             p.start()
@@ -423,14 +482,19 @@
                         jnp.where(lane_h == local, shares[e], 0.0), axis=1, keepdims=True
                     )
                     result = result + share * part_in[e, r].astype(jnp.float32)
-                out_ref[r] = result.astype(jnp.bfloat16)
+                heads_f32[swapped + r] = result
 
     for c in range(chunks):
         attend(c)
         if c:
             combine(c - 1)
     combine(chunks - 1)
-    for copy in list(sends.values()) + [copy for _, copy in outs]:
+    for h in range(heads):
+        att_ref[:, h * size : (h + 1) * size] = heads_f32[:, h, :].astype(jnp.bfloat16)
+
+    for copy in row_copies + tok_copies + list(sum_copies.values()) + ret_copies:
+        copy.wait_send()
+    for copy in swap_copies + list(sends.values()) + [copy for _, copy in outs]:
         copy.wait_send()
 
 
@@ -460,17 +524,8 @@
     before = (owner[:, None] == owner[None, :]) & (order[None, :] < order[:, None])
     place = owner * cap + jnp.sum(before.astype(jnp.int32), axis=1)
     cells = jnp.arange(n_ad * cap, dtype=jnp.int32)
-    pack = (cells[:, None] == place[None, :]).astype(jnp.bfloat16)
     unpack = (place[:, None] == cells[None, :]).astype(jnp.bfloat16)
-    marked = jnp.concatenate(
-        [
-            tokens,
-            jnp.broadcast_to((slots % held + 1).astype(jnp.bfloat16)[:, None], (rows, LANES)),
-        ],
-        axis=1,
-    )
-    packed = jnp.dot(pack, marked, preferred_element_type=jnp.float32).astype(jnp.bfloat16)
-    packed = packed.reshape(n_ad, cap, features + LANES)
+    mark = jnp.broadcast_to((slots % held + 1).astype(jnp.bfloat16)[:, None], (rows, LANES))
 
     half = head_dim // 2
     freq = jnp.exp(jnp.arange(half, dtype=jnp.float32) * (-2.0 * math.log(500000.0) / head_dim))
@@ -482,17 +537,25 @@
 
     depth = 1024
     slot_count = 4
+    swapped = SWAPPED
+    chunk = 32
+    heads = columns // head_dim
+    spread_rows = rows - swapped
+    chunks = spread_rows // chunk
+    kv_mine = kv_heads // n_tp
     vmem = pl.BlockSpec(memory_space=pltpu.VMEM)
+    smem = pl.BlockSpec(memory_space=pltpu.SMEM)
     anywhere = pl.BlockSpec(memory_space=pl.ANY)
     bf16, f32 = jnp.bfloat16, jnp.float32
     dma = pltpu.SemaphoreType.DMA
     groups = n_ad // 2
-    queries = pl.pallas_call(
-        functools.partial(query_kernel, n_ad, n_tp, cap, rank),
-        out_shape=jax.ShapeDtypeStruct((rows, columns), bf16),
-        in_specs=[vmem] * 5 + [anywhere] * 3,
-        out_specs=vmem,
+    return pl.pallas_call(
+        functools.partial(step_kernel, n_ad, n_tp, cap, rank, swapped, chunk),
+        out_shape=(jax.ShapeDtypeStruct((rows, columns), bf16),) * 2,
+        in_specs=[vmem] * 6 + [smem] + [anywhere] * 5,
+        out_specs=(vmem, vmem),
         scratch_shapes=[
+            pltpu.VMEM((n_ad, cap, features + LANES), bf16),
             pltpu.VMEM((n_tp, rows, features), bf16),
             pltpu.VMEM((n_ad, cap, features + LANES), bf16),
             pltpu.VMEM((n_ad, cap, columns), bf16),
@@ -501,12 +564,21 @@
             pltpu.VMEM((groups, n_tp, cap, LANES), f32),
             pltpu.VMEM((rows, columns), f32),
             pltpu.VMEM((slot_count, depth, columns), bf16),
-            pltpu.VMEM((held, features, rank), bf16),
-            pltpu.VMEM((held * rank // 256, features, 256), bf16),
+            pltpu.VMEM((held * rank, features), bf16),
             pltpu.VMEM((held * rank, columns), bf16),
+            pltpu.VMEM((rows, heads, head_dim), f32),
+            pltpu.VMEM((rows, heads, head_dim), bf16),
+            pltpu.VMEM((swapped, n_tp, kv_mine, span, head_dim), bf16),
+            pltpu.VMEM((swapped, n_tp, kv_mine, span, head_dim), bf16),
+            pltpu.VMEM((n_tp, spread_rows, heads, head_dim), bf16),
+            pltpu.VMEM((spread_rows, kv_heads, span, head_dim), bf16),
+            pltpu.VMEM((spread_rows, kv_heads, span, head_dim), bf16),
+            pltpu.VMEM((n_tp, spread_rows, heads, head_dim), bf16),
+            pltpu.VMEM((chunks, n_tp, heads, LANES), f32),
+            pltpu.VMEM((n_tp, spread_rows, heads, head_dim), bf16),
+            pltpu.VMEM((chunks, n_tp, heads, LANES), f32),
             dma((slot_count,)),
-            dma((held // 2,)),
-            dma,
+            dma((6,)),
             dma((n_tp,)),
             dma((n_tp,)),
             dma((n_ad,)),
@@ -515,40 +587,8 @@
             dma((groups, n_tp)),
             dma((n_ad,)),
             dma((n_ad,)),
-        ],
-        compiler_params=pltpu.CompilerParams(
-            collective_id=0, has_side_effects=True, vmem_limit_bytes=60 * 1024 * 1024
-        ),
-        name="project",
-    )(
-        packed,
-        unpack,
-        tokens,
-        cos_full,
-        sin_full,
-        query_weight,
-        adapter_down_weight,
-        adapter_up_weight.reshape(held * rank, columns),
-    )
-
-    heads = columns // head_dim
-    chunk = 32
-    chunks = rows // chunk
-    attended = pl.pallas_call(
-        functools.partial(attend_kernel, n_tp, chunk, span, kv_heads),
-        out_shape=jax.ShapeDtypeStruct((rows, heads, head_dim), bf16),
-        in_specs=[pl.BlockSpec(memory_space=pltpu.SMEM), vmem] + [anywhere] * 2,
-        out_specs=vmem,
-        scratch_shapes=[
-            pltpu.VMEM((n_tp, rows, heads, head_dim), bf16),
-            pltpu.VMEM((rows, kv_heads * span, head_dim), bf16),
-            pltpu.VMEM((rows, kv_heads * span, head_dim), bf16),
-            pltpu.VMEM((n_tp, rows, heads, head_dim), bf16),
-            pltpu.VMEM((chunks, n_tp, heads, LANES), f32),
-            pltpu.VMEM((n_tp, rows, heads, head_dim), bf16),
-            pltpu.VMEM((chunks, n_tp, heads, LANES), f32),
-            dma((chunks,)),
-            dma((chunks,)),
+            dma((2, n_tp)),
+            dma((2, n_tp)),
             dma((chunks, n_tp)),
             dma((chunks, n_tp)),
             dma((chunks, n_tp)),
@@ -557,16 +597,23 @@
             dma((chunks, n_tp)),
         ],
         compiler_params=pltpu.CompilerParams(
-            collective_id=1, has_side_effects=True, vmem_limit_bytes=48 * 1024 * 1024
+            collective_id=0, has_side_effects=True, vmem_limit_bytes=60 * 1024 * 1024
         ),
-        name="attend",
+        name="step",
     )(
+        place[None, :],
+        mark,
+        unpack,
+        tokens,
+        cos_full,
+        sin_full,
         lengths,
-        queries.reshape(rows, heads, head_dim),
-        cached_key_rows.reshape(rows, kv_heads * span, head_dim),
-        cached_value_rows.reshape(rows, kv_heads * span, head_dim),
-    )
-    return (queries, attended.reshape(rows, columns))
+        query_weight,
+        adapter_down_weight.transpose(0, 2, 1).reshape(held * rank, features),
+        adapter_up_weight.reshape(held * rank, columns),
+        cached_key_rows,
+        cached_value_rows,
+    )
 
 
 def rotate(query, lengths):

time: 169 us -> 160 us (0.947)
  local copies, waits for them, and re-layouts: 13.5 us -> 4.45 us
  matrix products: 2.9 us -> 0 us
  Pallas kernels: 148 us -> 150 us
    unnamed x10 -> x2, local copies, waits for them, and re-layouts: 13.4 us -> 3.76 us
    dot_general x1 -> x0, matrix products: 2.9 us -> none  [fused_device(): jnp.dot(pack, marked, preferred_element_type=jnp.float32)]
    pallas_call x2 -> x1, Pallas kernels: 148 us -> 150 us  [fused_device(): pl.pallas_call(functools.partial(step_kernel, n_ad, n_tp, cap, rank, swap...]
where the time goes in v2:
time: 160 us
  Pallas kernels  150 us (94%)
  local copies, waits for them, and re-layouts  4.45 us (3%)
  other arithmetic  4.07 us (3%)
    pallas_call x1, Pallas kernels, fused_device(): pl.pallas_call(functools.partial(step_kernel, n_ad, n_tp, cap, rank, swap...  150 us
    unnamed x2, local copies, waits for them, and re-layouts  3.76 us

profile of v2, /device:TPU:0, one launch (start us, length us, event | category | flops | bytes accessed | tf_op | source)
XLA Modules:
  0.0 159.7 jit_solution(548618427115978660)
XLA Ops:
  0.6 0.8 select_reduce_fusion
  1.5 0.7 add_convert_fusion
  2.2 0.2 convert_reduce_fusion
  2.4 0.6 bitcast_add_fusion.place_ref
  2.9 0.7 broadcast_in_dim.16.mark_ref
  3.6 0.7 fusion.unpack_ref
  4.4 0.3 fusion.2
  4.7 0.7 pad_maximum_fusion
  5.4 150.5 %step.1 = (bf16[128,2048]{1,0:T(8,128)(2,1)}, bf16[128,2048]{1,0:T(8,128)(2,1)}) custom-call(s32[1,128]{1,0:T(1,128)} %bitcast_add_fusion.place_ref, bf16[128,128]{1,0:T(8,128)(2,1)} %broadcast_in_dim.16.mark_ref, bf16[128,384]{1,0:T(8,128)(2,1)} %fusion.unpack_ref, bf16[128,2048]{1,0:T(8,128)(2,1)} %tokens_ref.1, f32[128,128]{1,0:T(8,128)} %get-tuple-element.7.cos_ref, ...), custom_call_target="tpu_custom_call" | custom-call | tf_op jit(solution)/shard_map/step/pallas_call | solution.py:552
  155.9 1.9 %copy.13 = bf16[128,2048]{1,0:T(8,128)(2,1)} copy(bf16[128,2048]{1,0:T(8,128)(2,1)} %get-tuple-element.11) | data formatting | bytes 1048576
  157.8 1.9 %copy.14 = bf16[128,2048]{1,0:T(8,128)(2,1)} copy(bf16[128,2048]{1,0:T(8,128)(2,1)} %get-tuple-element.12) | data formatting | bytes 1048576
  (3 shorter events, 0.0 us)

commit v3 on v2

--- a/solution.py
+++ b/solution.py
@@ -10,7 +10,7 @@
 
 MESH = pl.DeviceIdType.MESH
 LANES = 128
-SWAPPED = 64
+SWAPPED = 32
 
 
 def remote(src, dst, send_sem, recv_sem, axis, peer):

time: 160 us -> 145 us (0.906)
  Pallas kernels: 150 us -> 135 us
    pallas_call x1, Pallas kernels: 150 us -> 135 us  [fused_device(): pl.pallas_call(functools.partial(step_kernel, n_ad, n_tp, cap, rank, swap...]
where the time goes in v3:
time: 145 us; the launch traced here: 144 us
  Pallas kernels  135 us (93%)
  local copies, waits for them, and re-layouts  4.45 us (3%)
  other arithmetic  4.07 us (3%)
    pallas_call x1, Pallas kernels, fused_device(): pl.pallas_call(functools.partial(step_kernel, n_ad, n_tp, cap, rank, swap...  135 us
    unnamed x2, local copies, waits for them, and re-layouts  3.76 us

profile of v3, /device:TPU:0, one launch (start us, length us, event | category | flops | bytes accessed | tf_op | source)
XLA Modules:
  0.0 144.3 jit_solution(2584285809069653600)
XLA Ops:
  0.6 0.8 select_reduce_fusion
  1.5 0.7 add_convert_fusion
  2.2 0.2 convert_reduce_fusion
  2.4 0.6 bitcast_add_fusion.place_ref
  2.9 0.7 broadcast_in_dim.16.mark_ref
  3.6 0.7 fusion.unpack_ref
  4.4 0.3 fusion.2
  4.7 0.7 pad_maximum_fusion
  5.4 135.1 %step.1 = (bf16[128,2048]{1,0:T(8,128)(2,1)}, bf16[128,2048]{1,0:T(8,128)(2,1)}) custom-call(s32[1,128]{1,0:T(1,128)} %bitcast_add_fusion.place_ref, bf16[128,128]{1,0:T(8,128)(2,1)} %broadcast_in_dim.16.mark_ref, bf16[128,384]{1,0:T(8,128)(2,1)} %fusion.unpack_ref, bf16[128,2048]{1,0:T(8,128)(2,1)} %tokens_ref.1, f32[128,128]{1,0:T(8,128)} %get-tuple-element.7.cos_ref, ...), custom_call_target="tpu_custom_call" | custom-call | tf_op jit(solution)/shard_map/step/pallas_call | solution.py:552
  140.5 1.9 %copy.13 = bf16[128,2048]{1,0:T(8,128)(2,1)} copy(bf16[128,2048]{1,0:T(8,128)(2,1)} %get-tuple-element.11) | data formatting | bytes 1048576
  142.4 1.9 %copy.14 = bf16[128,2048]{1,0:T(8,128)(2,1)} copy(bf16[128,2048]{1,0:T(8,128)(2,1)} %get-tuple-element.12) | data formatting | bytes 1048576
  (3 shorter events, 0.0 us)
